TPU v7x, 32 devices: a whole 2x2x4 slice. The times are simulated.
32 devices in a mesh: ctx: 16 (over z, x, core), fsdp: 2 (over y).
Axes of the slice: x: 2, y: 2, z: 4, core: 2. Of those that a mesh axis runs over, the one named last changes fastest.
Arguments:
- query_heads: bfloat16 [1024, 3072], P(('ctx', 'fsdp')), may hold values from -6 to 6
- kv_latent: bfloat16 [1024, 576], P(('ctx', 'fsdp')), may hold values from -800 to 800
- w_uk: bfloat16 [512, 2048], P('ctx', 'fsdp'), may hold values from -0.25 to 0.25
- w_uv: bfloat16 [512, 2048], P('ctx', 'fsdp'), may hold values from -0.25 to 0.25
- span_order: int32 [32], replicated, may hold values from 0 to 31, each once
Outputs:
- attn_out: bfloat16 [1024, 2048], P(('ctx', 'fsdp'))
Inputs may be any that keep to these rules, and one draw needn't show every extreme that they name: `span_order`: each span number appears exactly once.
All inputs are finite; a program needn't handle non-finite values.
Results may differ from a plain program's by a relative error of at most 0.01.
The roundings to bfloat16 on the way count: a program that leaves them out, or rounds other values in their place, can miss the bound.
Values may be sent and summed in bfloat16 or wider, within the bound.
A program may use at most 64 MiB of HBM per device.

v0:
```python
import math

import jax
import jax.numpy as jnp
from jax import lax
from jax.sharding import PartitionSpec as P

LATENT = 512
ROPE = 64
NOPE = 128
VDIM = 128
SPAN = 32


def lookup(entries, wanted):
    matches = wanted[:, None] == jnp.arange(entries.shape[0], dtype=jnp.int32)[None, :]
    return jnp.sum(jnp.where(matches, entries[None, :], 0), axis=1)


def position(span_order, row_ids):
    return lookup(span_order, row_ids // SPAN) * SPAN + row_ids % SPAN


def rotary_tables(position_ids):
    half_width = ROPE // 2
    frequency = 10000.0 ** (-jnp.arange(half_width, dtype=jnp.float32) / half_width)
    angles = position_ids.astype(jnp.float32)[:, None] * frequency[None, :]
    return (jnp.cos(angles), jnp.sin(angles))


def rotate(values, cos_table, sin_table):
    half_width = ROPE // 2
    values = values.astype(jnp.float32)
    first_half = values[..., :half_width]
    second_half = values[..., half_width:]
    turned = jnp.concatenate(
        [
            first_half * cos_table - second_half * sin_table,
            second_half * cos_table + first_half * sin_table,
        ],
        axis=-1,
    )
    return turned.astype(jnp.bfloat16)


def body(query_heads, kv_latent, w_uk, w_uv, span_order):
    ctx_index = lax.axis_index("ctx")
    fsdp_index = lax.axis_index("fsdp")
    fsdp_count = lax.axis_size("fsdp")
    local_count = kv_latent.shape[0]
    row_count = local_count * fsdp_count
    score_scale = 1.0 / math.sqrt(NOPE + ROPE)
    queries = lax.all_to_all(query_heads, "fsdp", split_axis=1, concat_axis=0, tiled=True)
    head_count = queries.shape[1] // (NOPE + ROPE)
    queries = queries.reshape(row_count, head_count, NOPE + ROPE)
    key_map, value_map = (
        lax.all_gather(w_uk, "ctx", axis=0, tiled=True),
        lax.all_gather(w_uv, "ctx", axis=0, tiled=True),
    )
    query_pos = position(span_order, ctx_index * row_count + jnp.arange(row_count, dtype=jnp.int32))
    own_ids = (
        ctx_index * row_count + fsdp_index * local_count + jnp.arange(local_count, dtype=jnp.int32)
    )
    own_cos, own_sin = rotary_tables(position(span_order, own_ids))
    local_keys = jnp.concatenate(
        [kv_latent[:, :LATENT], rotate(kv_latent[:, LATENT:], own_cos, own_sin)], axis=1
    )
    query_cos, query_sin = rotary_tables(query_pos)
    query_latent = jnp.einsum(
        "rhd,nhd->rhn",
        queries[:, :, :NOPE],
        key_map.reshape(LATENT, head_count, NOPE),
        preferred_element_type=jnp.float32,
    ).astype(jnp.bfloat16)
    query_rope = rotate(queries[:, :, NOPE:], query_cos[:, None, :], query_sin[:, None, :])
    query_full = jnp.concatenate([query_latent, query_rope], axis=2)
    segment = lax.all_gather(local_keys, ("ctx", "fsdp"), axis=0, tiled=True)
    key_pos = position(span_order, jnp.arange(segment.shape[0], dtype=jnp.int32))
    row_max = jnp.full((row_count, head_count), -1e30, jnp.float32)
    totals = jnp.zeros((row_count, head_count), jnp.float32)
    accum = jnp.zeros((row_count, head_count, LATENT), jnp.float32)
    seg_count = segment.shape[0]
    for sub_begin in range(0, seg_count, 1024):
        sub_keys = segment[sub_begin : sub_begin + 1024]
        sub_pos = key_pos[sub_begin : sub_begin + 1024]
        allowed = (sub_pos[None, :] <= query_pos[:, None])[:, None, :]
        score_block = (
            jnp.einsum("rhe,ke->rhk", query_full, sub_keys, preferred_element_type=jnp.float32)
            * score_scale
        )
        score_block = jnp.where(allowed, score_block, jnp.float32(-1e30))
        new_max = jnp.maximum(row_max, jnp.max(score_block, axis=2))
        exp_vals = jnp.where(allowed, jnp.exp(score_block - new_max[:, :, None]), jnp.float32(0.0))
        rescale = jnp.exp(row_max - new_max)
        totals = totals * rescale + jnp.sum(exp_vals, axis=2)
        accum = accum * rescale[:, :, None] + jnp.einsum(
            "rhk,kn->rhn",
            exp_vals.astype(jnp.bfloat16),
            sub_keys[:, :LATENT],
            preferred_element_type=jnp.float32,
        )
        row_max = new_max
    row_max, totals, accum = (row_max, totals, accum)
    out_latent = (accum / totals[:, :, None]).astype(jnp.bfloat16)
    head_out = jnp.einsum(
        "rhn,nhd->rhd",
        out_latent,
        value_map.reshape(LATENT, head_count, VDIM),
        preferred_element_type=jnp.float32,
    ).astype(jnp.bfloat16)
    head_out = head_out.reshape(row_count, head_count * VDIM)
    return lax.all_to_all(head_out, "fsdp", split_axis=0, concat_axis=1, tiled=True)


def solution(mesh):
    placed = (
        P(("ctx", "fsdp"), None),
        P(("ctx", "fsdp"), None),
        P("ctx", "fsdp"),
        P("ctx", "fsdp"),
        P(),
    )
    return jax.shard_map(
        body, mesh=mesh, in_specs=placed, out_specs=P(("ctx", "fsdp"), None), check_vma=False
    )
```

profile of v0, /device:TPU:0, one launch (start us, length us, event | category | flops | bytes accessed | tf_op | source)
XLA Modules:
  0.0 166.3 jit_solution(8451803332605785282)
XLA Ops:
  6.5 0.0 all-gather.4.cloned.1.call-start
  6.5 0.7 all-gather.4.cloned.1.call-update
  7.3 0.0 all-gather.8.cloned.1.call-start
  7.3 0.7 all-gather.8.cloned.1.call-update
  8.0 0.0 all-gather.6.cloned.1.call-start
  8.1 0.8 slice.31
  8.8 0.8 select_reduce_fusion.1
  9.7 0.7 slice_convert_fusion
  10.4 0.1 fusion.22
  10.5 0.7 pad_maximum_fusion.1
  11.2 0.0 all-gather.6.cloned.1.call-update
  11.3 1.6 copy.105
  12.9 4.2 %all-to-all-start = ((bf16[32,2,1536]{2,0,1:T(8,128)(2,1)}), bf16[32,2,1536]{2,0,1:T(8,128)(2,1)S(1)}, u32[]{:S(2)}, u32[]{:S(2)}) async-start(bf16[32,2,1536]{2,0,1:T(8,128)(2,1)} %bitcast.24), calls=%async_computation | async-start | bytes 393216 | tf_op jit(solution)/shard_map/all_to_all | solution.py:53
  17.1 0.7 select_reduce_fusion.2
  17.9 0.7 select_reduce_fusion
  18.7 0.1 broadcast_compare_fusion
  18.8 0.2 multiply_cosine_fusion
  19.0 3.3 %all-to-all-done = bf16[32,2,1536]{2,0,1:T(8,128)(2,1)S(1)} async-done(((bf16[32,2,1536]{2,0,1:T(8,128)(2,1)}), bf16[32,2,1536]{2,0,1:T(8,128)(2,1)S(1)}, u32[]{:S(2)}, u32[]{:S(2)}) %all-to-all-start) | async-done | bytes 196640 | tf_op jit(solution)/shard_map/all_to_all | solution.py:53
  22.3 0.2 reshape.213
  22.6 0.1 subtract_convert_fusion
  22.7 27.5 %all-gather.4.cloned.1.call-done = bf16[512,1024]{1,0:T(8,128)(2,1)} async-done(((bf16[32,1024]{1,0:T(8,128)(2,1)}), bf16[512,1024]{1,0:T(8,128)(2,1)}) %all-gather.4.cloned.1.call-update) | async-done | bytes 1048592 | tf_op jit(solution)/shard_map/all_gather | solution.py:57
  50.2 1.5 copy.74
  51.7 37.5 %all-gather.8.cloned.1.call-done = bf16[512,1024]{1,0:T(8,128)(2,1)} async-done(((bf16[32,1024]{1,0:T(8,128)(2,1)}), bf16[512,1024]{1,0:T(8,128)(2,1)}) %all-gather.8.cloned.1.call-update) | async-done | bytes 1048592 | tf_op jit(solution)/shard_map/all_gather | solution.py:58
  89.2 2.3 %copy.84 = bf16[512,1024]{0,1:T(8,128)(2,1)} copy(bf16[512,1024]{1,0:T(8,128)(2,1)} %all-gather.8.cloned.1.call-done) | data formatting | bytes 2097152 | tf_op jit(solution)/shard_map/all_gather | solution.py:58
  91.5 0.3 fusion.7
  91.8 0.1 pad_maximum_fusion
  91.9 53.5 %all-gather.6.cloned.1.call-done = bf16[1024,576]{1,0:T(8,128)(2,1)} async-done(((bf16[32,576]{1,0:T(8,128)(2,1)}), bf16[1024,576]{1,0:T(8,128)(2,1)}) %all-gather.6.cloned.1.call-update) | async-done | bytes 1179664 | tf_op jit(solution)/shard_map/all_gather | solution.py:77
  145.4 2.6 %fusion = (f32[64,8]{1,0:T(8,128)S(1)}, f32[64,8,1024]{2,1,0:T(8,128)S(1)}) fusion(pred[64,1024]{1,0:T(8,128)(4,1)S(1)} %broadcast_compare_fusion, bf16[1024,576]{1,0:T(8,128)(2,1)} %all-gather.6.cloned.1.call-done, bf16[64,8,576]{2,0,1:T(8,128)(2,1)S(1)} %pad_maximum_fusion), kind=kOutput, calls=%fused_computation.2 | convolution fusion | flops 605552128 | bytes 3934208 | tf_op jit(solution)/shard_map/rhe,ke->rhk/dot_general | solution.py:88
  148.1 0.1 copy.80
  148.1 0.1 copy.81
  148.2 0.8 fusion.1
  149.1 0.1 copy.83
  149.1 2.7 %fusion.10 = bf16[64,8,128]{2,0,1:T(8,128)(2,1)S(1)} fusion(bf16[512,8,128]{0,2,1:T(8,128)(2,1)} %bitcast.26, bf16[1024,576]{1,0:T(8,128)(2,1)} %all-gather.6.cloned.1.call-done, bf16[64,8,1024]{2,1,0:T(8,128)(2,1)S(1)} %get-tuple-element.8, f32[64,8]{0,1:T(8,128)S(1)} %get-tuple-element.14, f32[64,8]{0,1:T(8,128)S(1)} %get-tuple-element.13), kind=kOutput, calls=%fused_computation.14 | convolution fusion | flops 604831744 | bytes 3280896 | tf_op jit(solution)/shard_map/rhn,nhd->rhd/dot_general | solution.py:105
  151.9 0.1 copy.86
  152.0 0.1 all_to_all.29
  152.1 7.0 %all_to_all.35 = bf16[2,32,1024]{2,1,0:T(8,128)(2,1)S(1)} all-to-all(bf16[2,32,1024]{2,1,0:T(8,128)(2,1)S(1)} %all_to_all.29), channel_id=1, replica_groups=mesh['ctx'=16,'fsdp'=2] {'fsdp'}, dimensions={0} | all-to-all | bytes 262144 | tf_op jit(solution)/shard_map/all_to_all | solution.py:112
  159.1 0.7 copy.93
  (12 shorter events, 0.1 us)
Async XLA Ops:
  6.5 43.7 %all-gather.4.cloned.1.call-start = ((), (), s32[]{:S(2)}) async-start(), calls=%async_computation.2 | async-start | bytes 1114112 | tf_op jit(solution)/shard_map/all_gather | solution.py:57
  7.3 82.0 %all-gather.8.cloned.1.call-start = ((), (), s32[]{:S(2)}) async-start(), calls=%async_computation.4 | async-start | bytes 1114112 | tf_op jit(solution)/shard_map/all_gather | solution.py:58
  8.0 137.4 %all-gather.6.cloned.1.call-start = ((), (), s32[]{:S(2)}) async-start(), calls=%async_computation.3 | async-start | bytes 1351680 | tf_op jit(solution)/shard_map/all_gather | solution.py:77
  12.9 9.4 %all-to-all-start = ((bf16[32,2,1536]{2,0,1:T(8,128)(2,1)}), bf16[32,2,1536]{2,0,1:T(8,128)(2,1)S(1)}, u32[]{:S(2)}, u32[]{:S(2)}) async-start(bf16[32,2,1536]{2,0,1:T(8,128)(2,1)} %bitcast.24), calls=%async_computation | async-start | bytes 393216 | tf_op jit(solution)/shard_map/all_to_all | solution.py:53
Sparse Core Ops, SparseCore 0:
  9.5 40.6 all-gather.3
  52.3 36.8 all-gather.7
  92.1 53.3 all-gather.5
where the time goes:
time: 167 us; the launch traced here: 166 us
  waiting for transfers between devices  123 us (74%)
  between operations  13.2 us (8%)
  local copies, waits for them, and re-layouts  7.41 us (4%)
  blocking collectives  7.04 us (4%)
  matrix products  5.68 us (3%)
  other arithmetic  5.37 us (3%)
  starting transfers between devices  4.31 us (3%)
    all_gather x1, waiting for transfers between devices, body(): segment = lax.all_gather(local_keys, ('ctx', 'fsdp'), axis=0, tiled=True)  53.5 us
    all_gather x1, waiting for transfers between devices, body(): lax.all_gather(w_uv, 'ctx', axis=0, tiled=True)  37.5 us
    all_gather x1, waiting for transfers between devices, body(): lax.all_gather(w_uk, 'ctx', axis=0, tiled=True)  27.5 us
    all_to_all x1, blocking collectives, body(): lax.all_to_all(head_out, 'fsdp', split_axis=0, concat_axis=1, tiled=True)  7.04 us
    all_to_all x1, starting transfers between devices, body(): lax.all_to_all(query_heads, 'fsdp', split_axis=1, concat_axis=0, tiled=True)  4.23 us
  transfers between devices with their start and end apart: 4, of which 4 were waited for; matrix products, arithmetic and copies ran while one was open for 7% of the time, Pallas kernels for 0%

commit v1 on v0

--- a/solution.py
+++ b/solution.py
@@ -1,8 +1,12 @@
+import functools
 import math
 
 import jax
 import jax.numpy as jnp
+import numpy as np
 from jax import lax
+from jax.experimental import pallas as pl
+from jax.experimental.pallas import tpu as pltpu
 from jax.sharding import PartitionSpec as P
 
 LATENT = 512
@@ -112,6 +116,347 @@
     return lax.all_to_all(head_out, "fsdp", split_axis=0, concat_axis=1, tiled=True)
 
 
+MESH = pl.DeviceIdType.MESH
+
+
+def rope_table(count):
+    half_width = ROPE // 2
+    frequency = np.float32(10000.0) ** (-np.arange(half_width, dtype=np.float32) / half_width)
+    angles = np.arange(count, dtype=np.float32)[:, None] * frequency[None, :].astype(np.float32)
+    cos, sin = np.cos(angles), np.sin(angles)
+    return np.concatenate([cos, cos, -sin, sin], axis=1).astype(np.float32)
+
+
+def turn(values, table):
+    half_width = ROPE // 2
+    values = values.astype(jnp.float32)
+    swapped = jnp.concatenate([values[:, half_width:], values[:, :half_width]], axis=1)
+    return (values * table[:, :ROPE] + swapped * table[:, ROPE:]).astype(jnp.bfloat16)
+
+
+def kernel(
+    span, q, kv, wuk, wuv, tab, out,
+    qb, kb, wkb, wvb, ob,
+    loc, ks, kr, sks, skr, wxs, wxr, wzs, wr, wss, wsr, qs, qr, os_, or_,
+):
+    depth = kb.shape[0]
+    heads = 4
+    width = heads * NOPE
+    q_width = heads * (NOPE + ROPE)
+    ctx = lax.axis_index("ctx")
+    f = lax.axis_index("fsdp")
+    c = lax.rem(ctx, 2)
+    x = lax.rem(lax.div(ctx, 2), 2)
+    z = lax.div(ctx, 4)
+
+    def dev(z_, x_, c_, f_):
+        return ((z_ * 2 + x_) * 2 + c_, f_)
+
+    plane = [(1 - x, f), (x, 1 - f), (1 - x, 1 - f)]
+    cols = [(x, f)] + plane
+    peers = [dev(z, px, c, pf) for px, pf in plane]
+    sib = dev(z, x, 1 - c, f)
+    up = dev(z + 1, x, c, f)
+    down = dev(z - 1, x, c, f)
+    has_up = z < depth - 1
+    has_down = z > 0
+
+    def rc(src, dst, ssem, rsem, device):
+        return pltpu.make_async_remote_copy(
+            src_ref=src, dst_ref=dst, send_sem=ssem, recv_sem=rsem,
+            device_id=device, device_id_type=MESH,
+        )
+
+    def lanes(index, size):
+        return pl.ds(pl.multiple_of(index * size, 128), size)
+
+    group = f * 2 + x
+    me = x * 2 + f
+    own = [
+        pltpu.make_async_copy(wuk.at[:, lanes(x, width)], wkb.at[z, x, c], loc.at[0]),
+        pltpu.make_async_copy(wuv.at[:, lanes(x, width)], wvb.at[z, x, c], loc.at[1]),
+        pltpu.make_async_copy(q.at[:, lanes(group, q_width)], qb.at[me], loc.at[2]),
+    ]
+
+    barrier = pltpu.get_barrier_semaphore()
+    for device in peers + [sib]:
+        pl.semaphore_signal(barrier, inc=1, device_id=device, device_id_type=MESH)
+
+    @pl.when(has_up)
+    def _():
+        pl.semaphore_signal(barrier, inc=1, device_id=up, device_id_type=MESH)
+
+    @pl.when(has_down)
+    def _():
+        pl.semaphore_signal(barrier, inc=1, device_id=down, device_id_type=MESH)
+
+    for copy in own:
+        copy.start()
+    own_tab = tab[span[ctx * 2 + f]]
+    kb[z, x, c, f, :, :LATENT] = kv[:, :LATENT]
+    kb[z, x, c, f, :, LATENT:] = turn(kv[:, LATENT:], own_tab)
+
+    pl.semaphore_wait(barrier, 4 + lax.min(z, 1) + lax.min(depth - 1 - z, 1))
+
+    def k_up(zi):
+        block = kb.at[zi, x, c, f]
+        return rc(block, block, ks.at[zi, 0], kr.at[zi, 0], up)
+
+    def k_down(zi):
+        block = kb.at[zi, x, c, f]
+        return rc(block, block, ks.at[zi, 1], kr.at[zi, 0], down)
+
+    def k_plane(zi, kind):
+        block = kb.at[zi, x, c, f]
+        return rc(block, block, ks.at[zi, 2 + kind], kr.at[zi, 1 + kind], peers[kind])
+
+    def k_plane_in(zi, kind):
+        block = kb.at[zi, plane[kind][0], c, plane[kind][1]]
+        return rc(block, block, ks.at[zi, 2 + kind], kr.at[zi, 1 + kind], peers[kind])
+
+    def k_sib(col, core):
+        block = kb.at[:, cols[col][0], core, cols[col][1]]
+        return rc(block, block, sks.at[col], skr.at[col], sib)
+
+    sources = (wuk, wuv)
+    bufs = (wkb, wvb)
+
+    def w_x(m):
+        return rc(
+            sources[m].at[:, lanes(1 - x, width)], bufs[m].at[z, x, c], wxs.at[m], wxr.at[m], peers[0]
+        )
+
+    def w_up(m, zi):
+        block = bufs[m].at[zi, :, c]
+        return rc(block, block, wzs.at[m, zi, 0], wr.at[m, zi], up)
+
+    def w_down(m, zi):
+        block = bufs[m].at[zi, :, c]
+        return rc(block, block, wzs.at[m, zi, 1], wr.at[m, zi], down)
+
+    def w_sib(m, zi, core):
+        block = bufs[m].at[zi, :, core]
+        return rc(block, block, wss.at[m, zi], wsr.at[m, zi], sib)
+
+    def q_send(kind):
+        px, pf = plane[kind]
+        return rc(
+            q.at[:, lanes(pf * 2 + px, q_width)], qb.at[me], qs.at[kind], qr.at[kind], peers[kind]
+        )
+
+    def q_in(kind):
+        px, pf = plane[kind]
+        block = qb.at[px * 2 + pf]
+        return rc(block, block, qs.at[kind], qr.at[kind], peers[kind])
+
+    def each_round(step, on_low, on_high):
+        pl.when(z - step >= 0)(lambda: on_low(z - step))
+        pl.when(z + step < depth)(lambda: on_high(z + step))
+
+    def k_low(zi):
+        k_up(zi).wait_recv()
+        pl.when(has_up)(lambda: k_up(zi).start())
+        for kind in range(3):
+            k_plane(zi, kind).start()
+
+    def k_high(zi):
+        k_down(zi).wait_recv()
+        pl.when(has_down)(lambda: k_down(zi).start())
+        for kind in range(3):
+            k_plane(zi, kind).start()
+
+    def w_low(m, zi):
+        w_up(m, zi).wait_recv()
+        pl.when(has_up)(lambda: w_up(m, zi).start())
+        w_sib(m, zi, c).start()
+
+    def w_high(m, zi):
+        w_down(m, zi).wait_recv()
+        pl.when(has_down)(lambda: w_down(m, zi).start())
+        w_sib(m, zi, c).start()
+
+    def k_round(step):
+        each_round(step, k_low, k_high)
+
+    def w_round(m, step):
+        each_round(step, functools.partial(w_low, m), functools.partial(w_high, m))
+
+    def w_first(m):
+        rc(bufs[m].at[z, 1 - x, c], bufs[m].at[z, 1 - x, c], wxs.at[m], wxr.at[m], peers[0]).wait_recv()
+        pl.when(has_up)(lambda: w_up(m, z).start())
+        pl.when(has_down)(lambda: w_down(m, z).start())
+        w_sib(m, z, c).start()
+
+    w_x(0).start()
+    pl.when(has_up)(lambda: k_up(z).start())
+    pl.when(has_down)(lambda: k_down(z).start())
+    for kind in range(3):
+        k_plane(z, kind).start()
+    w_x(1).start()
+    for kind in range(3):
+        q_send(kind).start()
+    for copy in own:
+        copy.wait()
+    w_first(0)
+    k_round(1)
+    w_round(0, 1)
+    w_first(1)
+    for step in range(2, depth):
+        k_round(step)
+        w_round(0, step)
+    k_sib(0, c).start()
+    for kind in range(3):
+        for zi in range(depth):
+            k_plane_in(zi, kind).wait_recv()
+        k_sib(1 + kind, c).start()
+    w_round(1, 1)
+    for kind in range(3):
+        q_in(kind).wait_recv()
+    for zi in range(depth):
+        w_sib(0, zi, 1 - c).wait_recv()
+
+    rows = 4 * SPAN
+    tables = []
+    places = []
+    for px in range(2):
+        for pf in range(2):
+            held = span[((z * 2 + px) * 2 + c) * 2 + pf]
+            tables.append(tab[held])
+            places.append(held * SPAN + lax.broadcasted_iota(jnp.int32, (SPAN, 1), 0))
+    table = jnp.concatenate(tables, axis=0)
+    query_pos = jnp.concatenate(places, axis=0)
+    queries = qb[...].reshape(rows, q_width)
+    key_map = wkb[...].reshape(LATENT, width)
+    lat, rot = [], []
+    for head in range(heads):
+        begin = head * (NOPE + ROPE)
+        lat.append(
+            lax.dot_general(
+                queries[:, begin : begin + NOPE],
+                key_map[:, head * NOPE : (head + 1) * NOPE],
+                (((1,), (1,)), ((), ())),
+                preferred_element_type=jnp.float32,
+            ).astype(jnp.bfloat16)
+        )
+        rot.append(turn(queries[:, begin + NOPE : begin + NOPE + ROPE], table))
+    total_keys = depth * 8 * SPAN
+    lane = lax.broadcasted_iota(jnp.int32, (1, total_keys), 1)
+    key_pos = jnp.zeros((1, total_keys), jnp.int32)
+    for slot in range(depth * 8):
+        key_pos = jnp.where(lane // SPAN == slot, span[slot] * SPAN, key_pos)
+    key_pos = key_pos + lane % SPAN
+    allowed = key_pos <= query_pos
+
+    for step in range(2, depth):
+        w_round(1, step)
+    for col in range(4):
+        k_sib(col, 1 - c).wait_recv()
+
+    keys_lat = kb[:, :, :, :, :, :LATENT].reshape(total_keys, LATENT)
+    keys_rot = kb[:, :, :, :, :, LATENT:].reshape(total_keys, ROPE)
+    scale = 1.0 / math.sqrt(NOPE + ROPE)
+    outs = []
+    for pair in range(2):
+        pick = slice(2 * pair, 2 * pair + 2)
+        score = lax.dot_general(
+            jnp.concatenate(lat[pick], axis=0), keys_lat,
+            (((1,), (1,)), ((), ())), preferred_element_type=jnp.float32,
+        ) + lax.dot_general(
+            jnp.concatenate(rot[pick], axis=0), keys_rot,
+            (((1,), (1,)), ((), ())), preferred_element_type=jnp.float32,
+        )
+        score = jnp.where(
+            allowed[None], score.reshape(2, rows, total_keys) * scale, jnp.float32(-1e30)
+        ).reshape(2 * rows, total_keys)
+        expo = jnp.exp(score - jnp.max(score, axis=1, keepdims=True))
+        totals = jnp.sum(expo, axis=1, keepdims=True)
+        accum = jnp.dot(expo.astype(jnp.bfloat16), keys_lat, preferred_element_type=jnp.float32)
+        outs.append((accum * (1.0 / totals)).astype(jnp.bfloat16))
+
+    for zi in range(depth):
+        w_sib(1, zi, 1 - c).wait_recv()
+
+    value_map = wvb[...].reshape(LATENT, width)
+    for head in range(heads):
+        part = outs[head // 2][(head % 2) * rows : (head % 2 + 1) * rows]
+        ob[:, :, head * VDIM : (head + 1) * VDIM] = (
+            jnp.dot(
+                part, value_map[:, head * VDIM : (head + 1) * VDIM],
+                preferred_element_type=jnp.float32,
+            )
+            .astype(jnp.bfloat16)
+            .reshape(4, SPAN, VDIM)
+        )
+
+    def o_send(kind):
+        px, pf = plane[kind]
+        return rc(
+            ob.at[px * 2 + pf], out.at[:, lanes(group, width)], os_.at[kind], or_.at[kind], peers[kind]
+        )
+
+    def o_in(kind):
+        px, pf = plane[kind]
+        block = out.at[:, lanes(pf * 2 + px, width)]
+        return rc(block, block, os_.at[kind], or_.at[kind], peers[kind])
+
+    for kind in range(3):
+        o_send(kind).start()
+    mine = pltpu.make_async_copy(ob.at[me], out.at[:, lanes(group, width)], loc.at[0])
+    mine.start()
+
+    for zi in range(depth):
+        pl.when(jnp.logical_and(has_up, zi <= z))(lambda zi=zi: k_up(zi).wait_send())
+        pl.when(jnp.logical_and(has_down, zi >= z))(lambda zi=zi: k_down(zi).wait_send())
+        for kind in range(3):
+            k_plane(zi, kind).wait_send()
+        for m in range(2):
+            pl.when(jnp.logical_and(has_up, zi <= z))(lambda zi=zi, m=m: w_up(m, zi).wait_send())
+            pl.when(jnp.logical_and(has_down, zi >= z))(lambda zi=zi, m=m: w_down(m, zi).wait_send())
+            w_sib(m, zi, c).wait_send()
+    for m in range(2):
+        w_x(m).wait_send()
+    for col in range(4):
+        k_sib(col, c).wait_send()
+    for kind in range(3):
+        q_send(kind).wait_send()
+    mine.wait()
+    for kind in range(3):
+        o_in(kind).wait_recv()
+        o_send(kind).wait_send()
+
+
+def planned(query_heads, kv_latent, w_uk, w_uv, span_order):
+    depth = lax.axis_size("ctx") // 4
+    local_count = kv_latent.shape[0]
+    width = w_uk.shape[1] // 2
+    q_width = query_heads.shape[1] // 4
+    dma = pltpu.SemaphoreType.DMA
+    vmem = pl.BlockSpec(memory_space=pltpu.VMEM)
+    spans = span_order.shape[0]
+    table = jnp.asarray(rope_table(spans * SPAN).reshape(spans, SPAN, 2 * ROPE))
+    return pl.pallas_call(
+        kernel,
+        out_shape=jax.ShapeDtypeStruct((local_count, width * 4), jnp.bfloat16),
+        in_specs=[pl.BlockSpec(memory_space=pltpu.SMEM)] + [vmem] * 5,
+        out_specs=vmem,
+        scratch_shapes=[
+            pltpu.VMEM((4, SPAN, q_width), jnp.bfloat16),
+            pltpu.VMEM((depth, 2, 2, 2, SPAN, LATENT + ROPE), jnp.bfloat16),
+            pltpu.VMEM((depth, 2, 2, w_uk.shape[0], width), jnp.bfloat16),
+            pltpu.VMEM((depth, 2, 2, w_uk.shape[0], width), jnp.bfloat16),
+            pltpu.VMEM((4, SPAN, width), jnp.bfloat16),
+            dma((3,)),
+            dma((depth, 5)), dma((depth, 4)), dma((4,)), dma((4,)),
+            dma((2,)), dma((2,)), dma((2, depth, 2)), dma((2, depth)), dma((2, depth)), dma((2, depth)),
+            dma((3,)), dma((3,)), dma((3,)), dma((3,)),
+        ],
+        compiler_params=pltpu.CompilerParams(
+            collective_id=0, has_side_effects=True, vmem_limit_bytes=48 * 1024 * 1024
+        ),
+        name="mla_prefill",
+    )(span_order, query_heads, kv_latent, w_uk, w_uv, table)
+
+
 def solution(mesh):
     placed = (
         P(("ctx", "fsdp"), None),
@@ -120,6 +465,17 @@
         P("ctx", "fsdp"),
         P(),
     )
-    return jax.shard_map(
-        body, mesh=mesh, in_specs=placed, out_specs=P(("ctx", "fsdp"), None), check_vma=False
-    )
+    small = mesh.shape["fsdp"] == 2 and mesh.shape["ctx"] == 16
+
+    def program(query_heads, kv_latent, w_uk, w_uv, span_order):
+        fits = (
+            small
+            and query_heads.shape[1] == 16 * (NOPE + ROPE)
+            and query_heads.shape[0] == 32 * SPAN
+        )
+        return jax.shard_map(
+            planned if fits else body,
+            mesh=mesh, in_specs=placed, out_specs=P(("ctx", "fsdp"), None), check_vma=False,
+        )(query_heads, kv_latent, w_uk, w_uv, span_order)
+
+    return program

time: 167 us -> 37.5 us (0.22)
  waiting for transfers between devices: 123 us -> 0 us
  Pallas kernels: 0 us -> 31.5 us
  between operations: 13.2 us -> 0.02 us
  blocking collectives: 7.04 us -> 0 us
  matrix products: 5.68 us -> 0 us
  other arithmetic: 5.37 us -> 0 us
  starting transfers between devices: 4.31 us -> 0 us
  local copies, waits for them, and re-layouts: 7.41 us -> 5.74 us
    all_gather x3 -> x0, waiting for transfers between devices: 119 us -> none  [the longest x1 53.5 us: body(): segment = lax.all_gather(local_keys, ('ctx', 'fsdp'), axis=0, tiled=True)]
    pallas_call x0 -> x1, Pallas kernels: none -> 31.5 us  [planned(): pl.pallas_call(kernel, out_shape=jax.ShapeDtypeStruct((local_count, width...]
    all_to_all x1 -> x0, blocking collectives: 7.04 us -> none  [body(): lax.all_to_all(head_out, 'fsdp', split_axis=0, concat_axis=1, tiled=True)]
    unnamed x0 -> x13, local copies, waits for them, and re-layouts: none -> 5.74 us
    dot_general x3 -> x0, matrix products: 5.68 us -> none  [the longest x1 2.75 us: body(): jnp.einsum('rhn,nhd->rhd', out_latent, value_map.reshape(LATENT, head_cou...]
    all_to_all x1 -> x0, starting transfers between devices: 4.23 us -> none  [body(): lax.all_to_all(query_heads, 'fsdp', split_axis=1, concat_axis=0, tiled=True)]
    all_gather x2 -> x0, local copies, waits for them, and re-layouts: 3.77 us -> none  [the longest x1 2.27 us: body(): lax.all_gather(w_uv, 'ctx', axis=0, tiled=True)]
    all_to_all x1 -> x0, waiting for transfers between devices: 3.3 us -> none  [body(): lax.all_to_all(query_heads, 'fsdp', split_axis=1, concat_axis=0, tiled=True)]
  transfers between devices with their start and end apart: 4 -> 0, of which waited for: 4 -> 0; matrix products, arithmetic and copies ran while one was open for 7% -> 0% of each run, Pallas kernels for 0% -> 0%
where the time goes in v1:
time: 37.5 us; the launch traced here: 37.2 us
  Pallas kernels  31.5 us (84%)
  local copies, waits for them, and re-layouts  5.74 us (15%)
    pallas_call x1, Pallas kernels, planned(): pl.pallas_call(kernel, out_shape=jax.ShapeDtypeStruct((local_count, width...  31.5 us
    unnamed x13, local copies, waits for them, and re-layouts  5.74 us

profile of v1, /device:TPU:0, one launch (start us, length us, event | category | flops | bytes accessed | tf_op | source)
XLA Modules:
  0.0 37.2 jit_solution(13974722094074553724)
XLA Ops:
  0.0 0.0 copy-start
  0.0 1.0 %copy-done = f32[32,32,128]{2,1,0:T(8,128)S(1)} copy-done((f32[32,32,128]{2,1,0:T(8,128)S(1)}, f32[32,32,128]{2,1,0:T(8,128)}, u32[]{:S(2)}) %copy-start) | copy-done | bytes 524312
  1.0 0.0 copy-start.1
  1.0 0.9 %copy-done.1 = bf16[32,3072]{1,0:T(8,128)(2,1)S(1)} copy-done((bf16[32,3072]{1,0:T(8,128)(2,1)S(1)}, bf16[32,3072]{1,0:T(8,128)(2,1)}, u32[]{:S(2)}) %copy-start.1) | copy-done | bytes 196632
  2.0 0.0 copy-start.2
  2.0 0.8 %copy-done.2 = bf16[32,1024]{1,0:T(8,128)(2,1)S(1)} copy-done((bf16[32,1024]{1,0:T(8,128)(2,1)S(1)}, bf16[32,1024]{1,0:T(8,128)(2,1)}, u32[]{:S(2)}) %copy-start.2) | copy-done | bytes 65560
  2.8 0.0 copy-start.3
  2.8 0.8 %copy-done.3 = bf16[32,1024]{1,0:T(8,128)(2,1)S(1)} copy-done((bf16[32,1024]{1,0:T(8,128)(2,1)S(1)}, bf16[32,1024]{1,0:T(8,128)(2,1)}, u32[]{:S(2)}) %copy-start.3) | copy-done | bytes 65560
  3.6 0.0 copy-start.4
  3.7 0.8 %copy-done.4 = bf16[32,576]{1,0:T(8,128)(2,1)S(1)} copy-done((bf16[32,576]{1,0:T(8,128)(2,1)S(1)}, bf16[32,576]{1,0:T(8,128)(2,1)}, u32[]{:S(2)}) %copy-start.4) | copy-done | bytes 36888
  4.4 0.0 copy-start.5
  4.4 0.7 %copy-done.5 = s32[32]{0:T(128)S(1)} copy-done((s32[32]{0:T(128)S(1)}, s32[32]{0:T(128)}, u32[]{:S(2)}) %copy-start.5) | copy-done | bytes 152
  5.1 31.5 %mla_prefill.1 = bf16[32,2048]{1,0:T(8,128)(2,1)S(1)} custom-call(s32[32]{0:T(128)S(1)} %copy-done.5, bf16[32,3072]{1,0:T(8,128)(2,1)S(1)} %copy-done.1, bf16[32,576]{1,0:T(8,128)(2,1)S(1)} %copy-done.4, bf16[32,1024]{1,0:T(8,128)(2,1)S(1)} %copy-done.2, bf16[32,1024]{1,0:T(8,128)(2,1)S(1)} %copy-done.3, f32[32,32,128]{2,1,0:T(8,128)S(1)} %copy-done), custom_call_target="tpu_custom_call" | custom-call | tf_op jit(solution)/shard_map/mla_prefill/pallas_call | solution.py:437
  36.5 0.7 %copy.8 = bf16[32,2048]{1,0:T(8,128)(2,1)} copy(bf16[32,2048]{1,0:T(8,128)(2,1)S(1)} %mla_prefill.1) | data formatting | bytes 262144
Async XLA Ops:
  0.0 1.0 %copy-start = (f32[32,32,128]{2,1,0:T(8,128)S(1)}, f32[32,32,128]{2,1,0:T(8,128)}, u32[]{:S(2)}) copy-start(f32[32,32,128]{2,1,0:T(8,128)} %constant.2.clone.tab) | copy-start | bytes 1572868
  1.0 0.9 %copy-start.1 = (bf16[32,3072]{1,0:T(8,128)(2,1)S(1)}, bf16[32,3072]{1,0:T(8,128)(2,1)}, u32[]{:S(2)}) copy-start(bf16[32,3072]{1,0:T(8,128)(2,1)} %q.1) | copy-start | bytes 589828
  2.0 0.8 %copy-start.2 = (bf16[32,1024]{1,0:T(8,128)(2,1)S(1)}, bf16[32,1024]{1,0:T(8,128)(2,1)}, u32[]{:S(2)}) copy-start(bf16[32,1024]{1,0:T(8,128)(2,1)} %wuk.1) | copy-start | bytes 196612
  2.8 0.8 %copy-start.3 = (bf16[32,1024]{1,0:T(8,128)(2,1)S(1)}, bf16[32,1024]{1,0:T(8,128)(2,1)}, u32[]{:S(2)}) copy-start(bf16[32,1024]{1,0:T(8,128)(2,1)} %wuv.1) | copy-start | bytes 196612
  3.6 0.8 %copy-start.4 = (bf16[32,576]{1,0:T(8,128)(2,1)S(1)}, bf16[32,576]{1,0:T(8,128)(2,1)}, u32[]{:S(2)}) copy-start(bf16[32,576]{1,0:T(8,128)(2,1)} %kv.1) | copy-start | bytes 110596
  4.4 0.7 %copy-start.5 = (s32[32]{0:T(128)S(1)}, s32[32]{0:T(128)}, u32[]{:S(2)}) copy-start(s32[32]{0:T(128)} %span.1) | copy-start | bytes 388

commit v2 on v1

--- a/solution.py
+++ b/solution.py
@@ -119,24 +119,31 @@
 MESH = pl.DeviceIdType.MESH
 
 
-def rope_table(count):
+def rope_table(count, stride):
     half_width = ROPE // 2
-    frequency = np.float32(10000.0) ** (-np.arange(half_width, dtype=np.float32) / half_width)
-    angles = np.arange(count, dtype=np.float32)[:, None] * frequency[None, :].astype(np.float32)
+    frequency = 10000.0 ** (-np.arange(half_width, dtype=np.float64) / half_width)
+    angles = np.arange(count)[:, None] * stride * frequency[None, :]
     cos, sin = np.cos(angles), np.sin(angles)
-    return np.concatenate([cos, cos, -sin, sin], axis=1).astype(np.float32)
-
-
-def turn(values, table):
+    return np.concatenate([cos, cos, sin, sin], axis=1).astype(np.float32)
+
+
+def span_table(coarse, fine):
+    cos = coarse[:, :ROPE] * fine[:, :ROPE] - coarse[:, ROPE:] * fine[:, ROPE:]
+    sin = coarse[:, ROPE:] * fine[:, :ROPE] + coarse[:, :ROPE] * fine[:, ROPE:]
+    first = lax.broadcasted_iota(jnp.int32, sin.shape, 1) < ROPE // 2
+    return cos, jnp.where(first, -sin, sin)
+
+
+def turn(values, cos, sin):
     half_width = ROPE // 2
     values = values.astype(jnp.float32)
     swapped = jnp.concatenate([values[:, half_width:], values[:, :half_width]], axis=1)
-    return (values * table[:, :ROPE] + swapped * table[:, ROPE:]).astype(jnp.bfloat16)
+    return (values * cos + swapped * sin).astype(jnp.bfloat16)
 
 
 def kernel(
-    span, q, kv, wuk, wuv, tab, out,
-    qb, kb, wkb, wvb, ob,
+    span_hbm, q, kv, wuk, wuv, coarse_hbm, fine_hbm, out,
+    span, coarse, fine, qb, kb, wkb, wvb, ob,
     loc, ks, kr, sks, skr, wxs, wxr, wzs, wr, wss, wsr, qs, qr, os_, or_,
 ):
     depth = kb.shape[0]
@@ -172,12 +179,20 @@
 
     group = f * 2 + x
     me = x * 2 + f
+    early = [
+        pltpu.make_async_copy(kv, kb.at[z, x, c, f], loc.at[3]),
+        pltpu.make_async_copy(span_hbm, span, loc.at[4]),
+        pltpu.make_async_copy(coarse_hbm, coarse, loc.at[5]),
+        pltpu.make_async_copy(fine_hbm, fine, loc.at[6]),
+    ]
     own = [
         pltpu.make_async_copy(wuk.at[:, lanes(x, width)], wkb.at[z, x, c], loc.at[0]),
         pltpu.make_async_copy(wuv.at[:, lanes(x, width)], wvb.at[z, x, c], loc.at[1]),
         pltpu.make_async_copy(q.at[:, lanes(group, q_width)], qb.at[me], loc.at[2]),
     ]
 
+    for copy in early:
+        copy.start()
     barrier = pltpu.get_barrier_semaphore()
     for device in peers + [sib]:
         pl.semaphore_signal(barrier, inc=1, device_id=device, device_id_type=MESH)
@@ -192,9 +207,10 @@
 
     for copy in own:
         copy.start()
-    own_tab = tab[span[ctx * 2 + f]]
-    kb[z, x, c, f, :, :LATENT] = kv[:, :LATENT]
-    kb[z, x, c, f, :, LATENT:] = turn(kv[:, LATENT:], own_tab)
+    for copy in early:
+        copy.wait()
+    own_tab = span_table(coarse[span[ctx * 2 + f]], fine[...])
+    kb[z, x, c, f, :, LATENT:] = turn(kb[z, x, c, f, :, LATENT:], *own_tab)
 
     pl.semaphore_wait(barrier, 4 + lax.min(z, 1) + lax.min(depth - 1 - z, 1))
 
@@ -321,9 +337,9 @@
     for px in range(2):
         for pf in range(2):
             held = span[((z * 2 + px) * 2 + c) * 2 + pf]
-            tables.append(tab[held])
+            tables.append(span_table(coarse[held], fine[...]))
             places.append(held * SPAN + lax.broadcasted_iota(jnp.int32, (SPAN, 1), 0))
-    table = jnp.concatenate(tables, axis=0)
+    table = [jnp.concatenate(part, axis=0) for part in zip(*tables)]
     query_pos = jnp.concatenate(places, axis=0)
     queries = qb[...].reshape(rows, q_width)
     key_map = wkb[...].reshape(LATENT, width)
@@ -338,7 +354,7 @@
                 preferred_element_type=jnp.float32,
             ).astype(jnp.bfloat16)
         )
-        rot.append(turn(queries[:, begin + NOPE : begin + NOPE + ROPE], table))
+        rot.append(turn(queries[:, begin + NOPE : begin + NOPE + ROPE], *table))
     total_keys = depth * 8 * SPAN
     lane = lax.broadcasted_iota(jnp.int32, (1, total_keys), 1)
     key_pos = jnp.zeros((1, total_keys), jnp.int32)
@@ -433,28 +449,33 @@
     dma = pltpu.SemaphoreType.DMA
     vmem = pl.BlockSpec(memory_space=pltpu.VMEM)
     spans = span_order.shape[0]
-    table = jnp.asarray(rope_table(spans * SPAN).reshape(spans, SPAN, 2 * ROPE))
+    hbm = pl.BlockSpec(memory_space=pltpu.HBM)
+    coarse = jnp.asarray(rope_table(spans, SPAN).reshape(spans, 1, 2 * ROPE))
+    fine = jnp.asarray(rope_table(SPAN, 1))
     return pl.pallas_call(
         kernel,
         out_shape=jax.ShapeDtypeStruct((local_count, width * 4), jnp.bfloat16),
-        in_specs=[pl.BlockSpec(memory_space=pltpu.SMEM)] + [vmem] * 5,
+        in_specs=[hbm] * 7,
         out_specs=vmem,
         scratch_shapes=[
+            pltpu.SMEM((spans,), jnp.int32),
+            pltpu.VMEM((spans, 1, 2 * ROPE), jnp.float32),
+            pltpu.VMEM((SPAN, 2 * ROPE), jnp.float32),
             pltpu.VMEM((4, SPAN, q_width), jnp.bfloat16),
             pltpu.VMEM((depth, 2, 2, 2, SPAN, LATENT + ROPE), jnp.bfloat16),
             pltpu.VMEM((depth, 2, 2, w_uk.shape[0], width), jnp.bfloat16),
             pltpu.VMEM((depth, 2, 2, w_uk.shape[0], width), jnp.bfloat16),
             pltpu.VMEM((4, SPAN, width), jnp.bfloat16),
-            dma((3,)),
+            dma((7,)),
             dma((depth, 5)), dma((depth, 4)), dma((4,)), dma((4,)),
             dma((2,)), dma((2,)), dma((2, depth, 2)), dma((2, depth)), dma((2, depth)), dma((2, depth)),
             dma((3,)), dma((3,)), dma((3,)), dma((3,)),
         ],
         compiler_params=pltpu.CompilerParams(
-            collective_id=0, has_side_effects=True, vmem_limit_bytes=48 * 1024 * 1024
+            collective_id=0, has_side_effects=True, vmem_limit_bytes=60 * 1024 * 1024
         ),
         name="mla_prefill",
-    )(span_order, query_heads, kv_latent, w_uk, w_uv, table)
+    )(span_order, query_heads, kv_latent, w_uk, w_uv, coarse, fine)
 
 
 def solution(mesh):

time: 37.5 us -> 33.5 us (0.89)
  local copies, waits for them, and re-layouts: 5.74 us -> 1.57 us
    unnamed x13 -> x1, local copies, waits for them, and re-layouts: 5.74 us -> 1.57 us
where the time goes in v2:
time: 33.5 us; the launch traced here: 33.3 us
  Pallas kernels  31.7 us (95%)
  local copies, waits for them, and re-layouts  1.57 us (5%)
    pallas_call x1, Pallas kernels, planned(): pl.pallas_call(kernel, out_shape=jax.ShapeDtypeStruct((local_count, width...  31.7 us
    unnamed x1, local copies, waits for them, and re-layouts  1.57 us

profile of v2, /device:TPU:0, one launch (start us, length us, event | category | flops | bytes accessed | tf_op | source)
XLA Modules:
  0.0 33.3 jit_solution(13561209397005127288)
XLA Ops:
  0.0 31.7 %mla_prefill.1 = bf16[32,2048]{1,0:T(8,128)(2,1)} custom-call(s32[32]{0:T(128)} %span_hbm.1, bf16[32,3072]{1,0:T(8,128)(2,1)} %q.1, bf16[32,576]{1,0:T(8,128)(2,1)} %kv.1, bf16[32,1024]{1,0:T(8,128)(2,1)} %wuk.1, bf16[32,1024]{1,0:T(8,128)(2,1)} %wuv.1, f32[32,1,128]{2,1,0:T(1,128)} %constant.4.clone.coarse_hbm, f32[32,128]{1,0:T(8,128)} %constant.5.clone.fine_hbm), custom_call_target="tpu_custom_call" | custom-call | tf_op jit(solution)/shard_map/mla_prefill/pallas_call | solution.py:455
  31.7 1.6 %copy.9 = bf16[32,2048]{1,0:T(8,128)(2,1)} copy(bf16[32,2048]{1,0:T(8,128)(2,1)} %mla_prefill.1) | data formatting | bytes 262144

commit v3 on v2

--- a/solution.py
+++ b/solution.py
@@ -160,7 +160,6 @@
         return ((z_ * 2 + x_) * 2 + c_, f_)
 
     plane = [(1 - x, f), (x, 1 - f), (1 - x, 1 - f)]
-    cols = [(x, f)] + plane
     peers = [dev(z, px, c, pf) for px, pf in plane]
     sib = dev(z, x, 1 - c, f)
     up = dev(z + 1, x, c, f)
@@ -230,9 +229,9 @@
         block = kb.at[zi, plane[kind][0], c, plane[kind][1]]
         return rc(block, block, ks.at[zi, 2 + kind], kr.at[zi, 1 + kind], peers[kind])
 
-    def k_sib(col, core):
-        block = kb.at[:, cols[col][0], core, cols[col][1]]
-        return rc(block, block, sks.at[col], skr.at[col], sib)
+    def k_sib(zi, core):
+        block = kb.at[zi, :, core]
+        return rc(block, block, sks.at[zi], skr.at[zi], sib)
 
     sources = (wuk, wuv)
     bufs = (wkb, wvb)
@@ -242,13 +241,15 @@
             sources[m].at[:, lanes(1 - x, width)], bufs[m].at[z, x, c], wxs.at[m], wxr.at[m], peers[0]
         )
 
-    def w_up(m, zi):
-        block = bufs[m].at[zi, :, c]
-        return rc(block, block, wzs.at[m, zi, 0], wr.at[m, zi], up)
-
-    def w_down(m, zi):
-        block = bufs[m].at[zi, :, c]
-        return rc(block, block, wzs.at[m, zi, 1], wr.at[m, zi], down)
+    halves = (x, 1 - x)
+
+    def w_up(m, half, zi):
+        block = bufs[m].at[zi, halves[half], c]
+        return rc(block, block, wzs.at[m, half, zi, 0], wr.at[m, half, zi], up)
+
+    def w_down(m, half, zi):
+        block = bufs[m].at[zi, halves[half], c]
+        return rc(block, block, wzs.at[m, half, zi, 1], wr.at[m, half, zi], down)
 
     def w_sib(m, zi, core):
         block = bufs[m].at[zi, :, core]
@@ -281,51 +282,58 @@
         for kind in range(3):
             k_plane(zi, kind).start()
 
-    def w_low(m, zi):
-        w_up(m, zi).wait_recv()
-        pl.when(has_up)(lambda: w_up(m, zi).start())
-        w_sib(m, zi, c).start()
-
-    def w_high(m, zi):
-        w_down(m, zi).wait_recv()
-        pl.when(has_down)(lambda: w_down(m, zi).start())
-        w_sib(m, zi, c).start()
-
-    def k_round(step):
-        each_round(step, k_low, k_high)
-
-    def w_round(m, step):
-        each_round(step, functools.partial(w_low, m), functools.partial(w_high, m))
-
-    def w_first(m):
-        rc(bufs[m].at[z, 1 - x, c], bufs[m].at[z, 1 - x, c], wxs.at[m], wxr.at[m], peers[0]).wait_recv()
-        pl.when(has_up)(lambda: w_up(m, z).start())
-        pl.when(has_down)(lambda: w_down(m, z).start())
-        w_sib(m, z, c).start()
-
+    def w_low(m, half, zi):
+        w_up(m, half, zi).wait_recv()
+        pl.when(has_up)(lambda: w_up(m, half, zi).start())
+        if half:
+            w_sib(m, zi, c).start()
+
+    def w_high(m, half, zi):
+        w_down(m, half, zi).wait_recv()
+        pl.when(has_down)(lambda: w_down(m, half, zi).start())
+        if half:
+            w_sib(m, zi, c).start()
+
+    def k_plane_done(zi):
+        for kind in range(3):
+            k_plane_in(zi, kind).wait_recv()
+        k_sib(zi, c).start()
+
+    def w_first(m, half):
+        if half:
+            block = bufs[m].at[z, 1 - x, c]
+            rc(block, block, wxs.at[m], wxr.at[m], peers[0]).wait_recv()
+            w_sib(m, z, c).start()
+        pl.when(has_up)(lambda: w_up(m, half, z).start())
+        pl.when(has_down)(lambda: w_down(m, half, z).start())
+
+    order = [(0, 0), (1, 0), (0, 1), (1, 1)]
     w_x(0).start()
     pl.when(has_up)(lambda: k_up(z).start())
     pl.when(has_down)(lambda: k_down(z).start())
-    for kind in range(3):
-        k_plane(z, kind).start()
+    k_plane(z, 1).start()
     w_x(1).start()
-    for kind in range(3):
-        q_send(kind).start()
     for copy in own:
         copy.wait()
-    w_first(0)
-    k_round(1)
-    w_round(0, 1)
-    w_first(1)
-    for step in range(2, depth):
-        k_round(step)
-        w_round(0, step)
-    k_sib(0, c).start()
-    for kind in range(3):
-        for zi in range(depth):
-            k_plane_in(zi, kind).wait_recv()
-        k_sib(1 + kind, c).start()
-    w_round(1, 1)
+    w_first(0, 0)
+    w_first(1, 0)
+    q_send(1).start()
+    w_first(0, 1)
+    k_plane(z, 0).start()
+    k_plane(z, 2).start()
+    w_first(1, 1)
+    q_send(0).start()
+    q_send(2).start()
+    for step in range(1, depth):
+        each_round(step, k_low, k_high)
+        for m, half in order:
+            each_round(
+                step, functools.partial(w_low, m, half), functools.partial(w_high, m, half)
+            )
+        if step == 1:
+            k_plane_done(z)
+        else:
+            each_round(step - 1, k_plane_done, k_plane_done)
     for kind in range(3):
         q_in(kind).wait_recv()
     for zi in range(depth):
@@ -363,10 +371,9 @@
     key_pos = key_pos + lane % SPAN
     allowed = key_pos <= query_pos
 
-    for step in range(2, depth):
-        w_round(1, step)
-    for col in range(4):
-        k_sib(col, 1 - c).wait_recv()
+    each_round(depth - 1, k_plane_done, k_plane_done)
+    for zi in range(depth):
+        k_sib(zi, 1 - c).wait_recv()
 
     keys_lat = kb[:, :, :, :, :, :LATENT].reshape(total_keys, LATENT)
     keys_rot = kb[:, :, :, :, :, LATENT:].reshape(total_keys, ROPE)
@@ -426,13 +433,18 @@
         for kind in range(3):
             k_plane(zi, kind).wait_send()
         for m in range(2):
-            pl.when(jnp.logical_and(has_up, zi <= z))(lambda zi=zi, m=m: w_up(m, zi).wait_send())
-            pl.when(jnp.logical_and(has_down, zi >= z))(lambda zi=zi, m=m: w_down(m, zi).wait_send())
+            for half in range(2):
+                pl.when(jnp.logical_and(has_up, zi <= z))(
+                    lambda zi=zi, m=m, half=half: w_up(m, half, zi).wait_send()
+                )
+                pl.when(jnp.logical_and(has_down, zi >= z))(
+                    lambda zi=zi, m=m, half=half: w_down(m, half, zi).wait_send()
+                )
             w_sib(m, zi, c).wait_send()
     for m in range(2):
         w_x(m).wait_send()
-    for col in range(4):
-        k_sib(col, c).wait_send()
+    for zi in range(depth):
+        k_sib(zi, c).wait_send()
     for kind in range(3):
         q_send(kind).wait_send()
     mine.wait()
@@ -467,8 +479,8 @@
             pltpu.VMEM((depth, 2, 2, w_uk.shape[0], width), jnp.bfloat16),
             pltpu.VMEM((4, SPAN, width), jnp.bfloat16),
             dma((7,)),
-            dma((depth, 5)), dma((depth, 4)), dma((4,)), dma((4,)),
-            dma((2,)), dma((2,)), dma((2, depth, 2)), dma((2, depth)), dma((2, depth)), dma((2, depth)),
+            dma((depth, 5)), dma((depth, 4)), dma((depth,)), dma((depth,)),
+            dma((2,)), dma((2,)), dma((2, 2, depth, 2)), dma((2, 2, depth)), dma((2, depth)), dma((2, depth)),
             dma((3,)), dma((3,)), dma((3,)), dma((3,)),
         ],
         compiler_params=pltpu.CompilerParams(

time: 33.5 us -> 29.3 us (0.87)
  Pallas kernels: 31.7 us -> 27.6 us
    pallas_call x1, Pallas kernels: 31.7 us -> 27.6 us  [planned(): pl.pallas_call(kernel, out_shape=jax.ShapeDtypeStruct((local_count, width...]
where the time goes in v3:
time: 29.3 us; the launch traced here: 29.2 us
  Pallas kernels  27.6 us (94%)
  local copies, waits for them, and re-layouts  1.57 us (5%)
    pallas_call x1, Pallas kernels, planned(): pl.pallas_call(kernel, out_shape=jax.ShapeDtypeStruct((local_count, width...  27.6 us
    unnamed x1, local copies, waits for them, and re-layouts  1.57 us

profile of v3, /device:TPU:0, one launch (start us, length us, event | category | flops | bytes accessed | tf_op | source)
XLA Modules:
  0.0 29.2 jit_solution(17736002602166284102)
XLA Ops:
  0.0 27.6 %mla_prefill.1 = bf16[32,2048]{1,0:T(8,128)(2,1)} custom-call(s32[32]{0:T(128)} %span_hbm.1, bf16[32,3072]{1,0:T(8,128)(2,1)} %q.1, bf16[32,576]{1,0:T(8,128)(2,1)} %kv.1, bf16[32,1024]{1,0:T(8,128)(2,1)} %wuk.1, bf16[32,1024]{1,0:T(8,128)(2,1)} %wuv.1, f32[32,1,128]{2,1,0:T(1,128)} %constant.4.clone.coarse_hbm, f32[32,128]{1,0:T(8,128)} %constant.5.clone.fine_hbm), custom_call_target="tpu_custom_call" | custom-call | tf_op jit(solution)/shard_map/mla_prefill/pallas_call | solution.py:467
  27.6 1.6 %copy.9 = bf16[32,2048]{1,0:T(8,128)(2,1)} copy(bf16[32,2048]{1,0:T(8,128)(2,1)} %mla_prefill.1) | data formatting | bytes 262144

commit v4 on v3

--- a/solution.py
+++ b/solution.py
@@ -229,6 +229,14 @@
         block = kb.at[zi, plane[kind][0], c, plane[kind][1]]
         return rc(block, block, ks.at[zi, 2 + kind], kr.at[zi, 1 + kind], peers[kind])
 
+    def k_diag(zi):
+        block = kb.at[zi, 1 - x, c, f]
+        return rc(block, block, ks.at[zi, 4], kr.at[zi, 3], peers[1])
+
+    def k_diag_in(zi):
+        block = kb.at[zi, 1 - x, c, 1 - f]
+        return rc(block, block, ks.at[zi, 4], kr.at[zi, 3], peers[1])
+
     def k_sib(zi, core):
         block = kb.at[zi, :, core]
         return rc(block, block, sks.at[zi], skr.at[zi], sib)
@@ -273,13 +281,13 @@
     def k_low(zi):
         k_up(zi).wait_recv()
         pl.when(has_up)(lambda: k_up(zi).start())
-        for kind in range(3):
+        for kind in range(2):
             k_plane(zi, kind).start()
 
     def k_high(zi):
         k_down(zi).wait_recv()
         pl.when(has_down)(lambda: k_down(zi).start())
-        for kind in range(3):
+        for kind in range(2):
             k_plane(zi, kind).start()
 
     def w_low(m, half, zi):
@@ -294,9 +302,13 @@
         if half:
             w_sib(m, zi, c).start()
 
+    def k_pass(zi):
+        k_plane_in(zi, 0).wait_recv()
+        k_diag(zi).start()
+
     def k_plane_done(zi):
-        for kind in range(3):
-            k_plane_in(zi, kind).wait_recv()
+        k_plane_in(zi, 1).wait_recv()
+        k_diag_in(zi).wait_recv()
         k_sib(zi, c).start()
 
     def w_first(m, half):
@@ -320,12 +332,15 @@
     q_send(1).start()
     w_first(0, 1)
     k_plane(z, 0).start()
-    k_plane(z, 2).start()
     w_first(1, 1)
     q_send(0).start()
     q_send(2).start()
     for step in range(1, depth):
         each_round(step, k_low, k_high)
+        if step == 1:
+            k_pass(z)
+        else:
+            each_round(step - 1, k_pass, k_pass)
         for m, half in order:
             each_round(
                 step, functools.partial(w_low, m, half), functools.partial(w_high, m, half)
@@ -334,6 +349,7 @@
             k_plane_done(z)
         else:
             each_round(step - 1, k_plane_done, k_plane_done)
+    each_round(depth - 1, k_pass, k_pass)
     for kind in range(3):
         q_in(kind).wait_recv()
     for zi in range(depth):
@@ -378,7 +394,31 @@
     keys_lat = kb[:, :, :, :, :, :LATENT].reshape(total_keys, LATENT)
     keys_rot = kb[:, :, :, :, :, LATENT:].reshape(total_keys, ROPE)
     scale = 1.0 / math.sqrt(NOPE + ROPE)
-    outs = []
+    for zi in range(depth):
+        w_sib(1, zi, 1 - c).wait_recv()
+    value_map = wvb[...].reshape(LATENT, width)
+
+    def o_cols(index, pair):
+        half = width // 2
+        return pl.ds(pl.multiple_of(index * width + pair * half, 128), half)
+
+    def o_send(pair, kind):
+        px, pf = plane[kind]
+        return rc(
+            ob.at[pair, px * 2 + pf], out.at[:, o_cols(group, pair)],
+            os_.at[pair, kind], or_.at[pair, kind], peers[kind],
+        )
+
+    def o_in(pair, kind):
+        px, pf = plane[kind]
+        block = out.at[:, o_cols(pf * 2 + px, pair)]
+        return rc(block, block, os_.at[pair, kind], or_.at[pair, kind], peers[kind])
+
+    def o_own(pair):
+        return pltpu.make_async_copy(
+            ob.at[pair, me], out.at[:, o_cols(group, pair)], loc.at[pair]
+        )
+
     for pair in range(2):
         pick = slice(2 * pair, 2 * pair + 2)
         score = lax.dot_general(
@@ -394,44 +434,28 @@
         expo = jnp.exp(score - jnp.max(score, axis=1, keepdims=True))
         totals = jnp.sum(expo, axis=1, keepdims=True)
         accum = jnp.dot(expo.astype(jnp.bfloat16), keys_lat, preferred_element_type=jnp.float32)
-        outs.append((accum * (1.0 / totals)).astype(jnp.bfloat16))
-
-    for zi in range(depth):
-        w_sib(1, zi, 1 - c).wait_recv()
-
-    value_map = wvb[...].reshape(LATENT, width)
-    for head in range(heads):
-        part = outs[head // 2][(head % 2) * rows : (head % 2 + 1) * rows]
-        ob[:, :, head * VDIM : (head + 1) * VDIM] = (
-            jnp.dot(
-                part, value_map[:, head * VDIM : (head + 1) * VDIM],
-                preferred_element_type=jnp.float32,
+        latent = (accum * (1.0 / totals)).astype(jnp.bfloat16)
+        for turn_at in range(2):
+            head = 2 * pair + turn_at
+            ob[pair, :, :, turn_at * VDIM : (turn_at + 1) * VDIM] = (
+                jnp.dot(
+                    latent[turn_at * rows : (turn_at + 1) * rows],
+                    value_map[:, head * VDIM : (head + 1) * VDIM],
+                    preferred_element_type=jnp.float32,
+                )
+                .astype(jnp.bfloat16)
+                .reshape(4, SPAN, VDIM)
             )
-            .astype(jnp.bfloat16)
-            .reshape(4, SPAN, VDIM)
-        )
-
-    def o_send(kind):
-        px, pf = plane[kind]
-        return rc(
-            ob.at[px * 2 + pf], out.at[:, lanes(group, width)], os_.at[kind], or_.at[kind], peers[kind]
-        )
-
-    def o_in(kind):
-        px, pf = plane[kind]
-        block = out.at[:, lanes(pf * 2 + px, width)]
-        return rc(block, block, os_.at[kind], or_.at[kind], peers[kind])
-
-    for kind in range(3):
-        o_send(kind).start()
-    mine = pltpu.make_async_copy(ob.at[me], out.at[:, lanes(group, width)], loc.at[0])
-    mine.start()
+        for kind in (2, 0, 1):
+            o_send(pair, kind).start()
+        o_own(pair).start()
 
     for zi in range(depth):
         pl.when(jnp.logical_and(has_up, zi <= z))(lambda zi=zi: k_up(zi).wait_send())
         pl.when(jnp.logical_and(has_down, zi >= z))(lambda zi=zi: k_down(zi).wait_send())
-        for kind in range(3):
+        for kind in range(2):
             k_plane(zi, kind).wait_send()
+        k_diag(zi).wait_send()
         for m in range(2):
             for half in range(2):
                 pl.when(jnp.logical_and(has_up, zi <= z))(
@@ -447,10 +471,11 @@
         k_sib(zi, c).wait_send()
     for kind in range(3):
         q_send(kind).wait_send()
-    mine.wait()
-    for kind in range(3):
-        o_in(kind).wait_recv()
-        o_send(kind).wait_send()
+    for pair in range(2):
+        o_own(pair).wait()
+        for kind in range(3):
+            o_in(pair, kind).wait_recv()
+            o_send(pair, kind).wait_send()
 
 
 def planned(query_heads, kv_latent, w_uk, w_uv, span_order):
@@ -477,11 +502,11 @@
             pltpu.VMEM((depth, 2, 2, 2, SPAN, LATENT + ROPE), jnp.bfloat16),
             pltpu.VMEM((depth, 2, 2, w_uk.shape[0], width), jnp.bfloat16),
             pltpu.VMEM((depth, 2, 2, w_uk.shape[0], width), jnp.bfloat16),
-            pltpu.VMEM((4, SPAN, width), jnp.bfloat16),
+            pltpu.VMEM((2, 4, SPAN, width // 2), jnp.bfloat16),
             dma((7,)),
             dma((depth, 5)), dma((depth, 4)), dma((depth,)), dma((depth,)),
             dma((2,)), dma((2,)), dma((2, 2, depth, 2)), dma((2, 2, depth)), dma((2, depth)), dma((2, depth)),
-            dma((3,)), dma((3,)), dma((3,)), dma((3,)),
+            dma((3,)), dma((3,)), dma((2, 3)), dma((2, 3)),
         ],
         compiler_params=pltpu.CompilerParams(
             collective_id=0, has_side_effects=True, vmem_limit_bytes=60 * 1024 * 1024

time: 29.3 us -> 33.5 us (1.14)
  Pallas kernels: 27.6 us -> 31.7 us
    pallas_call x1, Pallas kernels: 27.6 us -> 31.7 us  [planned(): pl.pallas_call(kernel, out_shape=jax.ShapeDtypeStruct((local_count, width...]
where the time goes in v4:
time: 33.5 us; the launch traced here: 33.3 us
  Pallas kernels  31.7 us (95%)
  local copies, waits for them, and re-layouts  1.57 us (5%)
    pallas_call x1, Pallas kernels, planned(): pl.pallas_call(kernel, out_shape=jax.ShapeDtypeStruct((local_count, width...  31.7 us
    unnamed x1, local copies, waits for them, and re-layouts  1.57 us

profile of v4, /device:TPU:0, one launch (start us, length us, event | category | flops | bytes accessed | tf_op | source)
XLA Modules:
  0.0 33.3 jit_solution(5623797849415017331)
XLA Ops:
  0.0 31.7 %mla_prefill.1 = bf16[32,2048]{1,0:T(8,128)(2,1)} custom-call(s32[32]{0:T(128)} %span_hbm.1, bf16[32,3072]{1,0:T(8,128)(2,1)} %q.1, bf16[32,576]{1,0:T(8,128)(2,1)} %kv.1, bf16[32,1024]{1,0:T(8,128)(2,1)} %wuk.1, bf16[32,1024]{1,0:T(8,128)(2,1)} %wuv.1, f32[32,1,128]{2,1,0:T(1,128)} %constant.4.clone.coarse_hbm, f32[32,128]{1,0:T(8,128)} %constant.5.clone.fine_hbm), custom_call_target="tpu_custom_call" | custom-call | tf_op jit(solution)/shard_map/mla_prefill/pallas_call | solution.py:492
  31.7 1.6 %copy.9 = bf16[32,2048]{1,0:T(8,128)(2,1)} copy(bf16[32,2048]{1,0:T(8,128)(2,1)} %mla_prefill.1) | data formatting | bytes 262144

commit v5 on v3

--- a/solution.py
+++ b/solution.py
@@ -229,9 +229,9 @@
         block = kb.at[zi, plane[kind][0], c, plane[kind][1]]
         return rc(block, block, ks.at[zi, 2 + kind], kr.at[zi, 1 + kind], peers[kind])
 
-    def k_sib(zi, core):
-        block = kb.at[zi, :, core]
-        return rc(block, block, sks.at[zi], skr.at[zi], sib)
+    def k_sib(zi, core, half):
+        block = kb.at[zi, halves[half], core]
+        return rc(block, block, sks.at[zi, half], skr.at[zi, half], sib)
 
     sources = (wuk, wuv)
     bufs = (wkb, wvb)
@@ -295,9 +295,11 @@
             w_sib(m, zi, c).start()
 
     def k_plane_done(zi):
-        for kind in range(3):
+        k_plane_in(zi, 1).wait_recv()
+        k_sib(zi, c, 0).start()
+        for kind in (0, 2):
             k_plane_in(zi, kind).wait_recv()
-        k_sib(zi, c).start()
+        k_sib(zi, c, 1).start()
 
     def w_first(m, half):
         if half:
@@ -373,7 +375,8 @@
 
     each_round(depth - 1, k_plane_done, k_plane_done)
     for zi in range(depth):
-        k_sib(zi, 1 - c).wait_recv()
+        for half in range(2):
+            k_sib(zi, 1 - c, half).wait_recv()
 
     keys_lat = kb[:, :, :, :, :, :LATENT].reshape(total_keys, LATENT)
     keys_rot = kb[:, :, :, :, :, LATENT:].reshape(total_keys, ROPE)
@@ -444,7 +447,8 @@
     for m in range(2):
         w_x(m).wait_send()
     for zi in range(depth):
-        k_sib(zi, c).wait_send()
+        for half in range(2):
+            k_sib(zi, c, half).wait_send()
     for kind in range(3):
         q_send(kind).wait_send()
     mine.wait()
@@ -479,7 +483,7 @@
             pltpu.VMEM((depth, 2, 2, w_uk.shape[0], width), jnp.bfloat16),
             pltpu.VMEM((4, SPAN, width), jnp.bfloat16),
             dma((7,)),
-            dma((depth, 5)), dma((depth, 4)), dma((depth,)), dma((depth,)),
+            dma((depth, 5)), dma((depth, 4)), dma((depth, 2)), dma((depth, 2)),
             dma((2,)), dma((2,)), dma((2, 2, depth, 2)), dma((2, 2, depth)), dma((2, depth)), dma((2, depth)),
             dma((3,)), dma((3,)), dma((3,)), dma((3,)),
         ],

time: 29.3 us -> 29.5 us (level)
  no operation moved by 1% of the time
where the time goes in v5:
time: 29.5 us; the launch traced here: 29.4 us
  Pallas kernels  27.8 us (94%)
  local copies, waits for them, and re-layouts  1.57 us (5%)
    pallas_call x1, Pallas kernels, planned(): pl.pallas_call(kernel, out_shape=jax.ShapeDtypeStruct((local_count, width...  27.8 us
    unnamed x1, local copies, waits for them, and re-layouts  1.57 us

profile of v5, /device:TPU:0, one launch (start us, length us, event | category | flops | bytes accessed | tf_op | source)
XLA Modules:
  0.0 29.4 jit_solution(11368446657298686475)
XLA Ops:
  0.0 27.8 %mla_prefill.1 = bf16[32,2048]{1,0:T(8,128)(2,1)} custom-call(s32[32]{0:T(128)} %span_hbm.1, bf16[32,3072]{1,0:T(8,128)(2,1)} %q.1, bf16[32,576]{1,0:T(8,128)(2,1)} %kv.1, bf16[32,1024]{1,0:T(8,128)(2,1)} %wuk.1, bf16[32,1024]{1,0:T(8,128)(2,1)} %wuv.1, f32[32,1,128]{2,1,0:T(1,128)} %constant.4.clone.coarse_hbm, f32[32,128]{1,0:T(8,128)} %constant.5.clone.fine_hbm), custom_call_target="tpu_custom_call" | custom-call | tf_op jit(solution)/shard_map/mla_prefill/pallas_call | solution.py:471
  27.8 1.6 %copy.9 = bf16[32,2048]{1,0:T(8,128)(2,1)} copy(bf16[32,2048]{1,0:T(8,128)(2,1)} %mla_prefill.1) | data formatting | bytes 262144
